TPU v7x, 32 devices: a whole 2x2x4 slice. The times are simulated.
32 devices in a mesh: dp: 2 (over x), row: 4 (over z), col: 4 (over y, core).
Axes of the slice: x: 2, y: 2, z: 4, core: 2. Of those that a mesh axis runs over, the one named last changes fastest.
Arguments:
- hidden: bfloat16 [8192, 896], P(('dp', 'row'), 'col'), may hold values from -6 to 6
- segments: int32 [2, 4, 4, 256], P('dp', 'col', 'row'), may hold values from 0 to 3, never falling along the last dimension, each value on 1 to 128 neighbouring positions
- attn_gain: bfloat16 [2, 896], P(None, 'col'), may hold values from 0.5 to 1.5
- qkv_weight: bfloat16 [2, 896, 1152], P(None, 'col', 'row'), as said below
- qkv_bias: bfloat16 [2, 1152], P(None, 'row'), may hold values from -3 to 3
- out_weight: bfloat16 [2, 896, 896], P(None, 'row', 'col'), may hold values from -0.09375 to 0.09375
- mlp_gain: bfloat16 [2, 896], P(None, 'col'), may hold values from 0.5 to 1.5
- gate_up_weight: bfloat16 [2, 896, 2, 4864], P(None, 'col', None, 'row'), may hold values from -0.1875 to 0.1875
- down_weight: bfloat16 [2, 4864, 896], P(None, 'row', 'col'), may hold values from -0.15625 to 0.15625
- cotangent: bfloat16 [8192, 896], P(('dp', 'row'), 'col'), may hold values from -6 to 6
Outputs:
- result: bfloat16 [8192, 896], P(('dp', 'row'), 'col')
- grad_hidden: float32 [8192, 896], P(('dp', 'row'), 'col')
- attn_gain_grad: float32 [2, 896], P(None, 'col')
- qkv_weight_grad: float32 [2, 896, 1152], P(None, 'col', 'row')
- qkv_bias_grad: float32 [2, 1152], P(None, 'row')
- out_weight_grad: float32 [2, 896, 896], P(None, 'row', 'col')
- mlp_gain_grad: float32 [2, 896], P(None, 'col')
- gate_up_grad: float32 [2, 896, 2, 4864], P(None, 'col', None, 'row')
- down_grad: float32 [2, 4864, 896], P(None, 'row', 'col')
Inputs may be any that keep to these rules, and one draw needn't show every extreme that they name: `segments`: along each packed sequence of 256 tokens the numbers never fall; each number covers at most 128 tokens, and some covers exactly that many. `qkv_weight`: entries lie within 48 * 896 ** -0.5 in magnitude.
All inputs are finite; a program needn't handle non-finite values.
Results may differ from a plain program's by a relative error of at most 0.023.
Values may be sent and summed in bfloat16 or wider, within the bound.
A program may use at most 256 MiB of HBM per device.

v0:
```python
import math

import jax
import jax.numpy as jnp
from jax import lax
from jax.sharding import PartitionSpec as P

D = 896
HEADS = 14
KV = 2
HEAD = 64
LAYERS = 2


norm_eps = 1e-06
rope_base = 1000000.0


def as_sent(x):

    def short(part):
        return part.astype(jnp.bfloat16) if part.dtype == jnp.float32 else part

    return jax.tree.map(short, x)


def multiply(left_rows, right_matrix, transposed):
    if transposed:
        return lax.dot_general(
            left_rows, right_matrix, (((1,), (1,)), ((), ())), preferred_element_type=jnp.float32
        )
    return jnp.dot(left_rows, right_matrix, preferred_element_type=jnp.float32)


def inner_rows(left_rows, right_rows):
    return lax.dot_general(
        left_rows, right_rows, (((0,), (0,)), ((), ())), preferred_element_type=jnp.float32
    )


def gather_rows(values):
    return lax.all_gather(values, "row", axis=0, tiled=True)


def gather_cols(values):
    return lax.all_gather(values, "col", axis=0, tiled=True)


def reduce_cols(left_rows, right_matrix, transposed):
    share_rows = left_rows.shape[0] // lax.axis_size("col")

    def block_term(start_row, row_count):
        return multiply(left_rows, right_matrix, transposed)

    return lax.psum_scatter(
        block_term(jnp.int32(0), lax.axis_size("col") * share_rows),
        "col",
        scatter_dimension=0,
        tiled=True,
    )


def reduce_rows(left_rows, right_matrix, transposed):
    share_rows = left_rows.shape[0] // lax.axis_size("row")

    def block_term(start_row, row_count):
        return multiply(left_rows, right_matrix, transposed)

    return lax.psum_scatter(
        block_term(jnp.int32(0), lax.axis_size("row") * share_rows),
        "row",
        scatter_dimension=0,
        tiled=True,
    )


def seq_layout(values):
    return lax.all_to_all(values, "row", split_axis=0, concat_axis=1, tiled=True)


def col_layout(values):
    return lax.all_to_all(values, "row", split_axis=1, concat_axis=0, tiled=True)


def width_total(values):
    return lax.psum(values, "col")


def sum_weights(grad_terms):
    return jax.tree.map(lambda part: part.astype(jnp.float32), lax.psum(as_sent(grad_terms), "dp"))


def sum_gains(grad_terms):
    return lax.psum(grad_terms, ("dp", "row"))


def norm_forward(stream, norm_gain):
    squares = width_total(jnp.sum(stream * stream, axis=1))
    inverse = lax.rsqrt(squares / D + norm_eps)
    normed = (stream * inverse[:, None] * norm_gain).astype(jnp.bfloat16)
    return (normed, inverse)


def norm_backward(stream, inverse, norm_gain, grad_normed):
    scaled = stream * inverse[:, None]
    gain_part = jnp.sum(grad_normed * scaled, axis=0)
    weighted = grad_normed * norm_gain
    inner_sum = width_total(jnp.sum(weighted * stream, axis=1))
    grad_stream = (
        weighted * inverse[:, None]
        - stream * (inverse * inverse * inverse * inner_sum / D)[:, None]
    )
    return (grad_stream, gain_part)


def rope_tables(seg_vec):
    index_all = jnp.arange(seg_vec.shape[0], dtype=jnp.int32)
    starts = jnp.concatenate([jnp.ones((1,), jnp.bool_), seg_vec[1:] != seg_vec[:-1]])
    first_idx = lax.cummax(jnp.where(starts, index_all, 0), axis=0)
    positions = (index_all - first_idx).astype(jnp.float32)
    half_dim = HEAD // 2
    freqs = rope_base ** (-(jnp.arange(half_dim, dtype=jnp.float32) * 2.0 / HEAD))
    angles = positions[:, None] * freqs[None, :]
    return (jnp.cos(angles)[:, None, :], jnp.sin(angles)[:, None, :])


def rotate(values, cosine, sine_vals):
    half_dim = values.shape[-1] // 2
    first_half = values[..., :half_dim]
    second_half = values[..., half_dim:]
    return jnp.concatenate(
        [
            first_half * cosine - second_half * sine_vals,
            second_half * cosine + first_half * sine_vals,
        ],
        axis=-1,
    )


def head_layout(qkv_seq, cosine, sine_vals):
    length = qkv_seq.shape[0]
    kv_width = KV * HEAD
    queries = rotate(
        qkv_seq[:, :D].astype(jnp.float32).reshape(length, HEADS, HEAD), cosine, sine_vals
    ).astype(jnp.bfloat16)
    keys_rot = rotate(
        qkv_seq[:, D : D + kv_width].astype(jnp.float32).reshape(length, KV, HEAD),
        cosine,
        sine_vals,
    ).astype(jnp.bfloat16)
    values_all = qkv_seq[:, D + kv_width :].reshape(length, KV, HEAD)
    block_rows = min(length, 512)
    query_blocks = queries.reshape(length // block_rows, block_rows, KV, HEADS // KV, HEAD)
    return (query_blocks, jnp.transpose(keys_rot, (1, 0, 2)), jnp.transpose(values_all, (1, 0, 2)))


def masked_scores(query_blk, keys_t, seg_blk, seg_vec, row_index):
    score_scale = 1.0 / math.sqrt(HEAD)
    col_index = jnp.arange(seg_vec.shape[0], dtype=jnp.int32)
    scores = (
        jnp.einsum("qkgd,ksd->kgqs", query_blk, keys_t, preferred_element_type=jnp.float32)
        * score_scale
    )
    allowed = (seg_blk[:, None] == seg_vec[None, :]) & (row_index[:, None] >= col_index[None, :])
    return jnp.where(allowed[None, None], scores, -1e30)


def attend_forward(qkv_seq, seg_vec, cosine, sine_vals):
    query_blocks, keys_t, values_t = head_layout(qkv_seq, cosine, sine_vals)
    num_blocks = query_blocks.shape[0]
    block_rows = query_blocks.shape[1]
    seg_blocks = seg_vec.reshape(num_blocks, block_rows)
    row_blocks = jnp.arange(seg_vec.shape[0], dtype=jnp.int32).reshape(num_blocks, block_rows)

    def one_block(inputs):
        query_blk, seg_blk, row_index = inputs
        scores = masked_scores(query_blk, keys_t, seg_blk, seg_vec, row_index)
        row_max = jnp.max(scores, axis=-1, keepdims=True)
        exp_scores = jnp.exp(scores - row_max)
        exp_total = jnp.sum(exp_scores, axis=-1, keepdims=True)
        probs = (exp_scores / exp_total).astype(jnp.bfloat16)
        output = jnp.einsum("kgqs,ksd->qkgd", probs, values_t, preferred_element_type=jnp.float32)
        return (
            output.reshape(block_rows, D).astype(jnp.bfloat16),
            (row_max + jnp.log(exp_total))[..., 0],
        )

    outputs, log_norm = lax.map(one_block, (query_blocks, seg_blocks, row_blocks))
    return (outputs.reshape(-1, D), log_norm)


def attend_backward(qkv_seq, seg_vec, cosine, sine_vals, log_norm, grad_attn):
    score_scale = 1.0 / math.sqrt(HEAD)
    query_blocks, keys_t, values_t = head_layout(qkv_seq, cosine, sine_vals)
    num_blocks = query_blocks.shape[0]
    block_rows = query_blocks.shape[1]
    length = seg_vec.shape[0]
    seg_blocks = seg_vec.reshape(num_blocks, block_rows)
    row_blocks = jnp.arange(length, dtype=jnp.int32).reshape(num_blocks, block_rows)
    grad_blocks = grad_attn.reshape(num_blocks, block_rows, KV, HEADS // KV, HEAD)

    def one_block(carry, inputs):
        grad_keys, grad_values = carry
        query_blk, grad_blk, norm_blk, seg_blk, row_index = inputs
        scores = masked_scores(query_blk, keys_t, seg_blk, seg_vec, row_index)
        probs = jnp.exp(scores - norm_blk[..., None])
        grad_probs = jnp.einsum(
            "qkgd,ksd->kgqs", grad_blk, values_t, preferred_element_type=jnp.float32
        )
        inner_sum = jnp.sum(probs * grad_probs, axis=-1, keepdims=True)
        grad_scores = (probs * (grad_probs - inner_sum)).astype(jnp.bfloat16)
        grad_values = grad_values + jnp.einsum(
            "kgqs,qkgd->ksd",
            probs.astype(jnp.bfloat16),
            grad_blk,
            preferred_element_type=jnp.float32,
        )
        grad_keys = (
            grad_keys
            + jnp.einsum(
                "kgqs,qkgd->ksd", grad_scores, query_blk, preferred_element_type=jnp.float32
            )
            * score_scale
        )
        grad_query = (
            jnp.einsum("kgqs,ksd->qkgd", grad_scores, keys_t, preferred_element_type=jnp.float32)
            * score_scale
        )
        return ((grad_keys, grad_values), grad_query)

    zero_keys = jnp.zeros(keys_t.shape, jnp.float32)
    carried, grad_query = lax.scan(
        one_block,
        (zero_keys, zero_keys),
        (query_blocks, grad_blocks, log_norm, seg_blocks, row_blocks),
    )
    grad_keys, grad_values = carried
    grad_query = rotate(grad_query.reshape(length, HEADS, HEAD), cosine, -sine_vals)
    grad_keys = rotate(jnp.transpose(grad_keys, (1, 0, 2)), cosine, -sine_vals)
    grad_values = jnp.transpose(grad_values, (1, 0, 2))
    joined = jnp.concatenate(
        [
            grad_query.reshape(length, D),
            grad_keys.reshape(length, -1),
            grad_values.reshape(length, -1),
        ],
        axis=1,
    )
    return joined.astype(jnp.bfloat16)


def silu_product(gate_part, up_part):
    return jax.nn.silu(gate_part) * up_part


def on_device(
    hidden,
    segments,
    attn_gain,
    qkv_weight,
    qkv_bias,
    out_weight,
    mlp_gain,
    gate_up_weight,
    down_weight,
    cotangent,
):
    seg_vec = segments.reshape(-1)
    cosine, sine_vals = rope_tables(seg_vec)
    stream = hidden.astype(jnp.float32)
    width_dev = gate_up_weight.shape[1]
    saved_layers = []
    for layer_no in range(LAYERS):
        gain_attn = attn_gain[layer_no].astype(jnp.float32)
        gain_mlp = mlp_gain[layer_no].astype(jnp.float32)
        normed_a, inverse_a = norm_forward(stream, gain_attn)
        gathered_a = gather_rows(normed_a)
        qkv_part = reduce_cols(gathered_a, qkv_weight[layer_no], False)
        qkv_cols = (qkv_part + qkv_bias[layer_no].astype(jnp.float32)).astype(jnp.bfloat16)
        qkv_seq = seq_layout(qkv_cols)
        attn_seq, log_norm = attend_forward(qkv_seq, seg_vec, cosine, sine_vals)
        attn_cols = col_layout(attn_seq)
        gathered_o = gather_cols(attn_cols)
        stream_mid = stream + reduce_rows(gathered_o, out_weight[layer_no], False)
        normed_m, inverse_m = norm_forward(stream_mid, gain_mlp)
        gathered_m = gather_rows(normed_m)
        gate_flat = gate_up_weight[layer_no].reshape(width_dev, -1)
        gate_up = reduce_cols(gathered_m, gate_flat, False)
        ff_dev = gate_up.shape[1] // 2
        act_vals = silu_product(gate_up[:, :ff_dev], gate_up[:, ff_dev:]).astype(jnp.bfloat16)
        gathered_h = gather_cols(act_vals)
        stream_next = stream_mid + reduce_rows(gathered_h, down_weight[layer_no], False)
        stored = (gathered_a, gathered_o, gathered_m, gathered_h)
        saved_layers.append(
            (stream, inverse_a, qkv_seq, log_norm, stream_mid, inverse_m, gate_up, stored)
        )
        stream = stream_next
    outcome = stream.astype(jnp.bfloat16)
    grad_stream = cotangent.astype(jnp.float32)
    weight_list = []
    gain_list = []
    for layer_no in reversed(range(LAYERS)):
        stream_in, inverse_a, qkv_seq, log_norm, stream_mid, inverse_m, gate_up, stored = (
            saved_layers[layer_no]
        )
        gain_attn = attn_gain[layer_no].astype(jnp.float32)
        gain_mlp = mlp_gain[layer_no].astype(jnp.float32)
        gate_flat = gate_up_weight[layer_no].reshape(width_dev, -1)
        ff_dev = gate_up.shape[1] // 2
        grad_down = grad_stream.astype(jnp.bfloat16)
        gathered_d = gather_rows(grad_down)
        grad_act = reduce_cols(gathered_d, down_weight[layer_no], True)
        gathered_h = stored[3]
        w_down_grad = inner_rows(gathered_h, gathered_d)
        silu_out, silu_back = jax.vjp(silu_product, gate_up[:, :ff_dev], gate_up[:, ff_dev:])
        grad_gate, grad_up = silu_back(grad_act)
        grad_gu = jnp.concatenate([grad_gate, grad_up], axis=1).astype(jnp.bfloat16)
        gathered_g = gather_cols(grad_gu)
        grad_normed_m = reduce_rows(gathered_g, gate_flat, True)
        gathered_m = stored[2]
        w_gate_grad = inner_rows(gathered_m, gathered_g).reshape(width_dev, 2, ff_dev)
        grad_norm_m, gain_mlp_part = norm_backward(stream_mid, inverse_m, gain_mlp, grad_normed_m)
        grad_mid = grad_stream + grad_norm_m
        grad_out = grad_mid.astype(jnp.bfloat16)
        gathered_y = gather_rows(grad_out)
        grad_attn_cols = reduce_cols(gathered_y, out_weight[layer_no], True)
        gathered_o = stored[1]
        w_out_grad = inner_rows(gathered_o, gathered_y)
        grad_attn_seq = seq_layout(grad_attn_cols.astype(jnp.bfloat16))
        grad_qkv_seq = attend_backward(qkv_seq, seg_vec, cosine, sine_vals, log_norm, grad_attn_seq)
        grad_qkv_cols = col_layout(grad_qkv_seq)
        gathered_q = gather_cols(grad_qkv_cols)
        bias_grad = jnp.sum(gathered_q, axis=0, dtype=jnp.float32)
        grad_normed_a = reduce_rows(gathered_q, qkv_weight[layer_no], True)
        gathered_a = stored[0]
        w_qkv_grad = inner_rows(gathered_a, gathered_q)
        grad_norm_a, gain_attn_part = norm_backward(stream_in, inverse_a, gain_attn, grad_normed_a)
        grad_stream = grad_mid + grad_norm_a
        weight_terms = (w_qkv_grad, bias_grad, w_out_grad, w_gate_grad, w_down_grad)
        gain_terms = (gain_attn_part, gain_mlp_part)
        weight_list.insert(0, weight_terms)
        gain_list.insert(0, gain_terms)
    weight_stack = tuple(
        (jnp.stack([member[index_no] for member in weight_list]) for index_no in range(5))
    )
    gain_stack = tuple(
        (jnp.stack([member[index_no] for member in gain_list]) for index_no in range(2))
    )
    weight_stack = sum_weights(weight_stack)
    gain_stack = sum_gains(gain_stack)
    return (
        outcome,
        grad_stream,
        gain_stack[0],
        weight_stack[0],
        weight_stack[1],
        weight_stack[2],
        gain_stack[1],
        weight_stack[3],
        weight_stack[4],
    )


def solution(mesh):
    in_specs = (
        P(("dp", "row"), "col"),
        P("dp", "col", "row", None),
        P(None, "col"),
        P(None, "col", "row"),
        P(None, "row"),
        P(None, "row", "col"),
        P(None, "col"),
        P(None, "col", None, "row"),
        P(None, "row", "col"),
        P(("dp", "row"), "col"),
    )
    out_specs = (
        P(("dp", "row"), "col"),
        P(("dp", "row"), "col"),
        P(None, "col"),
        P(None, "col", "row"),
        P(None, "row"),
        P(None, "row", "col"),
        P(None, "col"),
        P(None, "col", None, "row"),
        P(None, "row", "col"),
    )
    return jax.shard_map(
        on_device, mesh=mesh, in_specs=in_specs, out_specs=out_specs, check_vma=False
    )
```

profile of v0, /device:TPU:0, one launch (start us, length us, event | category | flops | bytes accessed | tf_op | source)
XLA Modules:
  0.0 2898.0 jit_solution(12900651117420374474)
XLA Ops:
  8.4 8.4 psum.105
  19.5 41.7 %all-gather.17.cloned.1.call-done = bf16[4096,224]{0,1:T(8,128)(2,1)} async-done(((bf16[1024,224]{0,1:T(8,128)(2,1)}), bf16[4096,224]{0,1:T(8,128)(2,1)}) %all-gather.17.cloned.1.call-update) | async-done | bytes 1835024 | tf_op jit(solution)/shard_map/all_gather | solution.py:42
  67.1 45.5 %reduce-scatter.17.cloned.1.call-done = f32[1024,288]{0,1:T(8,128)} async-done(((f32[4096,288]{0,1:T(8,128)}), f32[1024,288]{0,1:T(8,128)}) %reduce-scatter.17.cloned.1.call-update) | async-done | bytes 1179664 | tf_op jit(solution)/shard_map/reduce_scatter | solution.py:55
  120.6 14.6 all-to-all-done
  138.9 15.0 all_to_all.134
  154.8 19.3 all-gather.19.cloned.1.call-done
  178.8 68.0 %reduce-scatter.19.cloned.1.call-done = f32[1024,224]{0,1:T(8,128)} async-done(((f32[4096,224]{0,1:T(8,128)}), f32[1024,224]{0,1:T(8,128)}) %reduce-scatter.19.cloned.1.call-update) | async-done | bytes 917520 | tf_op jit(solution)/shard_map/reduce_scatter | solution.py:69
  248.2 6.2 psum.106
  260.4 36.4 %all-gather.21.cloned.1.call-done = bf16[4096,224]{0,1:T(8,128)(2,1)} async-done(((bf16[1024,224]{0,1:T(8,128)(2,1)}), bf16[4096,224]{0,1:T(8,128)(2,1)}) %all-gather.21.cloned.1.call-update) | async-done | bytes 1835024 | tf_op jit(solution)/shard_map/all_gather | solution.py:42
  296.8 17.2 fusion.120
  314.3 268.9 %reduce-scatter.21.cloned.1.call-done = f32[1024,2432]{1,0:T(8,128)} async-done(((f32[4096,2432]{1,0:T(8,128)}), f32[1024,2432]{1,0:T(8,128)}) %reduce-scatter.21.cloned.1.call-update) | async-done | bytes 9961488 | tf_op jit(solution)/shard_map/reduce_scatter | solution.py:55
  583.2 6.1 multiply_convert_fusion.3
  589.4 70.3 %all-gather.23.cloned.1.call-done = bf16[4096,1216]{1,0:T(8,128)(2,1)} async-done(((bf16[1024,1216]{1,0:T(8,128)(2,1)}), bf16[4096,1216]{1,0:T(8,128)(2,1)}) %all-gather.23.cloned.1.call-update) | async-done | bytes 9961488 | tf_op jit(solution)/shard_map/all_gather | solution.py:46
  659.7 9.0 fusion.64
  668.8 68.7 %reduce-scatter.23.cloned.1.call-done = f32[1024,224]{0,1:T(8,128)} async-done(((f32[4096,224]{0,1:T(8,128)}), f32[1024,224]{0,1:T(8,128)}) %reduce-scatter.23.cloned.1.call-update) | async-done | bytes 917520 | tf_op jit(solution)/shard_map/reduce_scatter | solution.py:69
  738.8 6.2 psum.107
  745.9 41.4 %all-gather.25.cloned.1.call-done = bf16[4096,224]{0,1:T(8,128)(2,1)} async-done(((bf16[1024,224]{0,1:T(8,128)(2,1)}), bf16[4096,224]{0,1:T(8,128)(2,1)}) %all-gather.25.cloned.1.call-update) | async-done | bytes 1835024 | tf_op jit(solution)/shard_map/all_gather | solution.py:42
  791.9 46.7 %reduce-scatter.25.cloned.1.call-done = f32[1024,288]{0,1:T(8,128)} async-done(((f32[4096,288]{0,1:T(8,128)}), f32[1024,288]{0,1:T(8,128)}) %reduce-scatter.25.cloned.1.call-update) | async-done | bytes 1179664 | tf_op jit(solution)/shard_map/reduce_scatter | solution.py:55
  840.1 20.1 all_to_all.135
  863.2 14.9 all_to_all.136
  879.0 19.3 all-gather.27.cloned.1.call-done
  903.1 67.9 %reduce-scatter.27.cloned.1.call-done = f32[1024,224]{0,1:T(8,128)} async-done(((f32[4096,224]{0,1:T(8,128)}), f32[1024,224]{0,1:T(8,128)}) %reduce-scatter.27.cloned.1.call-update) | async-done | bytes 917520 | tf_op jit(solution)/shard_map/reduce_scatter | solution.py:69
  972.4 6.2 psum.108
  979.5 34.7 %all-gather.33.cloned.1.call-done = bf16[4096,224]{0,1:T(8,128)(2,1)} async-done(((bf16[1024,224]{0,1:T(8,128)(2,1)}), bf16[4096,224]{0,1:T(8,128)(2,1)}) %all-gather.33.cloned.1.call-update) | async-done | bytes 1835024 | tf_op jit(solution)/shard_map/all_gather | solution.py:42
  1014.2 12.0 fusion.58
  1029.3 27.1 all-gather.29.cloned.1.call-done
  1056.4 27.3 fusion.121
  1083.8 124.4 %reduce-scatter.33.cloned.1.call-done = f32[1024,1216]{1,0:T(8,128)} async-done(((f32[4096,1216]{1,0:T(8,128)}), f32[1024,1216]{1,0:T(8,128)}) %reduce-scatter.33.cloned.1.call-update) | async-done | bytes 4980752 | tf_op jit(solution)/shard_map/reduce_scatter | solution.py:55
  1208.2 272.7 %reduce-scatter.29.cloned.1.call-done = f32[1024,2432]{1,0:T(8,128)} async-done(((f32[4096,2432]{1,0:T(8,128)}), f32[1024,2432]{1,0:T(8,128)}) %reduce-scatter.29.cloned.1.call-update) | async-done | bytes 9961488 | tf_op jit(solution)/shard_map/reduce_scatter | solution.py:55
  1480.9 8.4 fusion.2
  1493.0 125.9 %all-gather.35.cloned.1.call-done = bf16[4096,2432]{1,0:T(8,128)(2,1)} async-done(((bf16[1024,2432]{1,0:T(8,128)(2,1)}), bf16[4096,2432]{1,0:T(8,128)(2,1)}) %all-gather.35.cloned.1.call-update) | async-done | bytes 19922960 | tf_op jit(solution)/shard_map/all_gather | solution.py:46
  1618.9 14.8 fusion.122
  1633.8 68.7 %reduce-scatter.35.cloned.1.call-done = f32[1024,224]{0,1:T(8,128)} async-done(((f32[4096,224]{0,1:T(8,128)}), f32[1024,224]{0,1:T(8,128)}) %reduce-scatter.35.cloned.1.call-update) | async-done | bytes 917520 | tf_op jit(solution)/shard_map/reduce_scatter | solution.py:69
  1704.4 6.7 psum.109
  1714.7 41.4 %all-gather.37.cloned.1.call-done = bf16[4096,224]{0,1:T(8,128)(2,1)} async-done(((bf16[1024,224]{0,1:T(8,128)(2,1)}), bf16[4096,224]{0,1:T(8,128)(2,1)}) %all-gather.37.cloned.1.call-update) | async-done | bytes 1835024 | tf_op jit(solution)/shard_map/all_gather | solution.py:42
  1760.2 40.1 %reduce-scatter.37.cloned.1.call-done = f32[1024,224]{0,1:T(8,128)} async-done(((f32[4096,224]{0,1:T(8,128)}), f32[1024,224]{0,1:T(8,128)}) %reduce-scatter.37.cloned.1.call-update) | async-done | bytes 917520 | tf_op jit(solution)/shard_map/reduce_scatter | solution.py:55
  1807.8 12.1 all-to-all-done.4
  1827.4 17.8 all_to_all.137
  1846.9 21.6 all-gather.39.cloned.1.call-done
  1873.2 67.0 %all-gather.31.cloned.1.call-done = bf16[4096,1216]{1,0:T(8,128)(2,1)} async-done(((bf16[1024,1216]{1,0:T(8,128)(2,1)}), bf16[4096,1216]{1,0:T(8,128)(2,1)}) %all-gather.31.cloned.1.call-update) | async-done | bytes 9961488 | tf_op jit(solution)/shard_map/all_gather | solution.py:46
  1940.2 9.1 fusion.60
  1949.4 62.3 %reduce-scatter.39.cloned.1.call-done = f32[1024,224]{0,1:T(8,128)} async-done(((f32[4096,224]{0,1:T(8,128)}), f32[1024,224]{0,1:T(8,128)}) %reduce-scatter.39.cloned.1.call-update) | async-done | bytes 917520 | tf_op jit(solution)/shard_map/reduce_scatter | solution.py:69
  2013.1 6.2 psum.110
  2019.3 63.4 %reduce-scatter.31.cloned.1.call-done = f32[1024,224]{0,1:T(8,128)} async-done(((f32[4096,224]{0,1:T(8,128)}), f32[1024,224]{0,1:T(8,128)}) %reduce-scatter.31.cloned.1.call-update) | async-done | bytes 917520 | tf_op jit(solution)/shard_map/reduce_scatter | solution.py:69
  2086.2 41.7 %all-gather.41.cloned.1.call-done = bf16[4096,224]{0,1:T(8,128)(2,1)} async-done(((bf16[1024,224]{0,1:T(8,128)(2,1)}), bf16[4096,224]{0,1:T(8,128)(2,1)}) %all-gather.41.cloned.1.call-update) | async-done | bytes 1835024 | tf_op jit(solution)/shard_map/all_gather | solution.py:42
  2127.9 11.6 fusion.62
  2139.9 149.1 %reduce-scatter.41.cloned.1.call-done = f32[1024,1216]{1,0:T(8,128)} async-done(((f32[4096,1216]{1,0:T(8,128)}), f32[1024,1216]{1,0:T(8,128)}) %reduce-scatter.41.cloned.1.call-update) | async-done | bytes 4980752 | tf_op jit(solution)/shard_map/reduce_scatter | solution.py:55
  2289.0 7.0 fusion.5
  2299.8 125.9 %all-gather.43.cloned.1.call-done = bf16[4096,2432]{1,0:T(8,128)(2,1)} async-done(((bf16[1024,2432]{1,0:T(8,128)(2,1)}), bf16[4096,2432]{1,0:T(8,128)(2,1)}) %all-gather.43.cloned.1.call-update) | async-done | bytes 19922960 | tf_op jit(solution)/shard_map/all_gather | solution.py:46
  2425.7 12.3 fusion.123
  2438.1 68.6 %reduce-scatter.43.cloned.1.call-done = f32[1024,224]{0,1:T(8,128)} async-done(((f32[4096,224]{0,1:T(8,128)}), f32[1024,224]{0,1:T(8,128)}) %reduce-scatter.43.cloned.1.call-update) | async-done | bytes 917520 | tf_op jit(solution)/shard_map/reduce_scatter | solution.py:69
  2508.1 6.2 psum.111
  2516.9 41.4 %all-gather.45.cloned.1.call-done = bf16[4096,224]{0,1:T(8,128)(2,1)} async-done(((bf16[1024,224]{0,1:T(8,128)(2,1)}), bf16[4096,224]{0,1:T(8,128)(2,1)}) %all-gather.45.cloned.1.call-update) | async-done | bytes 1835024 | tf_op jit(solution)/shard_map/all_gather | solution.py:42
  2562.4 40.0 %reduce-scatter.45.cloned.1.call-done = f32[1024,224]{0,1:T(8,128)} async-done(((f32[4096,224]{0,1:T(8,128)}), f32[1024,224]{0,1:T(8,128)}) %reduce-scatter.45.cloned.1.call-update) | async-done | bytes 917520 | tf_op jit(solution)/shard_map/reduce_scatter | solution.py:55
  2609.0 7.4 fusion.19
  2616.4 5.6 all-to-all-done.6
  2632.7 10.3 convolution_convert_fusion
  2651.0 7.2 fusion.18
  2659.4 10.4 convolution_convert_fusion.1
  2672.8 6.6 pad_maximum_fusion.2
  2698.2 90.3 %all-reduce.4.cloned.1.call-done = (bf16[2,224,288]{1,2,0:T(8,128)(2,1)}, bf16[2,224,224]{2,1,0:T(8,128)(2,1)}, bf16[2,224,2,1216]{3,2,1,0:T(2,128)(2,1)}, bf16[2,1216,224]{1,2,0:T(8,128)(2,1)}) async-done(((bf16[2,224,288]{1,2,0:T(8,128)(2,1)}, bf16[2,224,224]{2,1,0:T(8,128)(2,1)}, bf16[2,224,2,1216]{3,2,1,0:T(2,128)(2,1)}, bf16[2,1216,224]{1,2,0:T(8,128)(2,1)}), (bf16[2,224,288]{1,2,0:T(8,128)(2,1)}, ...) | async-done | bytes 3727376 | tf_op jit(solution)/shard_map/psum | solution.py:90
  2797.3 62.1 %reduce-scatter.47.cloned.1.call-done = f32[1024,224]{0,1:T(8,128)} async-done(((f32[4096,224]{0,1:T(8,128)}), f32[1024,224]{0,1:T(8,128)}) %reduce-scatter.47.cloned.1.call-update) | async-done | bytes 917520 | tf_op jit(solution)/shard_map/reduce_scatter | solution.py:69
  2860.8 6.1 psum.112
  2867.0 21.6 all-reduce
  (365 shorter events, 169.3 us)
Async XLA Ops:
  7.2 54.1 %all-gather.17.cloned.1.call-start = ((), (), s32[]{:S(2)}) async-start(), calls=%async_computation.24 | async-start | bytes 2293760 | tf_op jit(solution)/shard_map/all_gather | solution.py:42
  17.5 727.4 %copy-start.75 = (f32[1,224]{1,0:T(1,128)}, f32[1,224]{1,0:T(1,128)S(1)}, u32[]{:S(2)}) copy-start(f32[1,224]{1,0:T(1,128)S(1)} %get-tuple-element.194) | copy-start | bytes 2692
  19.5 93.1 %reduce-scatter.17.cloned.1.call-start = ((), (), s32[]{:S(2)}) async-start(), calls=%async_computation.25 | async-start | bytes 5898240 | tf_op jit(solution)/shard_map/reduce_scatter | solution.py:55
  114.9 20.3 all-to-all-start
  119.5 54.6 %all-gather.19.cloned.1.call-start = ((), (), s32[]{:S(2)}) async-start(), calls=%async_computation.26 | async-start | bytes 2293760 | tf_op jit(solution)/shard_map/all_gather | solution.py:46
  154.7 92.1 %reduce-scatter.19.cloned.1.call-start = ((), (), s32[]{:S(2)}) async-start(), calls=%async_computation.27 | async-start | bytes 4587520 | tf_op jit(solution)/shard_map/reduce_scatter | solution.py:69
  178.1 68.7 %copy-start.5 = (bf16[1024,224]{0,1:T(8,128)(2,1)S(1)}, bf16[1024,224]{0,1:T(8,128)(2,1)}, u32[]{:S(2)}) copy-start(bf16[1024,224]{0,1:T(8,128)(2,1)} %param.10) | copy-start | bytes 1376260
  178.1 118.7 %all-gather.21.cloned.1.call-start = ((), (), s32[]{:S(2)}) async-start(), calls=%async_computation.28 | async-start | bytes 2293760 | tf_op jit(solution)/shard_map/all_gather | solution.py:42
  178.8 80.8 %copy-start.77 = (f32[1,224]{1,0:T(1,128)}, f32[1,224]{1,0:T(1,128)S(1)}, u32[]{:S(2)}) copy-start(f32[1,224]{1,0:T(1,128)S(1)} %get-tuple-element.193) | copy-start | bytes 2692
  178.8 1533.0 %copy-start.73 = (f32[1,224]{1,0:T(1,128)}, f32[1,224]{1,0:T(1,128)S(1)}, u32[]{:S(2)}) copy-start(f32[1,224]{1,0:T(1,128)S(1)} %get-tuple-element.192) | copy-start | bytes 2692
  255.3 327.9 %reduce-scatter.21.cloned.1.call-start = ((), (), s32[]{:S(2)}) async-start(), calls=%async_computation.29 | async-start | bytes 49807360 | tf_op jit(solution)/shard_map/reduce_scatter | solution.py:55
  260.4 53.6 %copy-start.8 = (bf16[224,2432]{1,0:T(8,128)(2,1)}, bf16[224,2432]{1,0:T(8,128)(2,1)S(1)}, u32[]{:S(2)}) copy-start(bf16[224,2432]{1,0:T(8,128)(2,1)S(1)} %reshape_squeeze.8) | copy-start | bytes 3268612
  314.1 345.6 %copy-start.20 = (bf16[2,1216,224]{1,2,0:T(8,128)(2,1)S(1)}, bf16[2,1216,224]{1,2,0:T(8,128)(2,1)}, u32[]{:S(2)}) copy-start(bf16[2,1216,224]{1,2,0:T(8,128)(2,1)} %param.18) | copy-start | bytes 3268612
  314.1 345.6 %all-gather.23.cloned.1.call-start = ((), (), s32[]{:S(2)}) async-start(), calls=%async_computation.30 | async-start | bytes 13107200 | tf_op jit(solution)/shard_map/all_gather | solution.py:46
  589.3 148.1 %reduce-scatter.23.cloned.1.call-start = ((), (), s32[]{:S(2)}) async-start(), calls=%async_computation.31 | async-start | bytes 4587520 | tf_op jit(solution)/shard_map/reduce_scatter | solution.py:69
  668.7 118.7 %copy-start.18 = (bf16[2,224,288]{1,2,0:T(8,128)(2,1)S(1)}, bf16[2,224,288]{1,2,0:T(8,128)(2,1)}, u32[]{:S(2)}) copy-start(bf16[2,224,288]{1,2,0:T(8,128)(2,1)} %param.13) | copy-start | bytes 774148
  668.7 118.7 %all-gather.25.cloned.1.call-start = ((), (), s32[]{:S(2)}) async-start(), calls=%async_computation.32 | async-start | bytes 2293760 | tf_op jit(solution)/shard_map/all_gather | solution.py:42
  745.9 92.7 %reduce-scatter.25.cloned.1.call-start = ((), (), s32[]{:S(2)}) async-start(), calls=%async_computation.33 | async-start | bytes 5898240 | tf_op jit(solution)/shard_map/reduce_scatter | solution.py:55
  791.9 106.4 %all-gather.27.cloned.1.call-start = ((), (), s32[]{:S(2)}) async-start(), calls=%async_computation.34 | async-start | bytes 2293760 | tf_op jit(solution)/shard_map/all_gather | solution.py:46
  878.9 92.1 %reduce-scatter.27.cloned.1.call-start = ((), (), s32[]{:S(2)}) async-start(), calls=%async_computation.35 | async-start | bytes 4587520 | tf_op jit(solution)/shard_map/reduce_scatter | solution.py:69
  902.3 111.9 %all-gather.33.cloned.1.call-start = ((), (), s32[]{:S(2)}) async-start(), calls=%async_computation.40 | async-start | bytes 2293760 | tf_op jit(solution)/shard_map/all_gather | solution.py:42
  903.1 153.3 %all-gather.29.cloned.1.call-start = ((), (), s32[]{:S(2)}) async-start(), calls=%async_computation.36 | async-start | bytes 2293760 | tf_op jit(solution)/shard_map/all_gather | solution.py:42
  978.5 733.3 %copy-start.49 = (f32[1024]{0:T(1024)}, f32[1024]{0:T(1024)S(1)}, u32[]{:S(2)}) copy-start(f32[1024]{0:T(1024)S(1)} %add_rsqrt_fusion) | copy-start | bytes 12292
  979.5 228.8 %reduce-scatter.33.cloned.1.call-start = ((), (), s32[]{:S(2)}) async-start(), calls=%async_computation.41 | async-start | bytes 26214400 | tf_op jit(solution)/shard_map/reduce_scatter | solution.py:55
  1026.2 454.7 %reduce-scatter.29.cloned.1.call-start = ((), (), s32[]{:S(2)}) async-start(), calls=%async_computation.37 | async-start | bytes 49807360 | tf_op jit(solution)/shard_map/reduce_scatter | solution.py:55
  1083.8 535.1 %all-gather.35.cloned.1.call-start = ((), (), s32[]{:S(2)}) async-start(), calls=%async_computation.42 | async-start | bytes 24903680 | tf_op jit(solution)/shard_map/all_gather | solution.py:46
  1493.0 209.5 %reduce-scatter.35.cloned.1.call-start = ((), (), s32[]{:S(2)}) async-start(), calls=%async_computation.43 | async-start | bytes 4587520 | tf_op jit(solution)/shard_map/reduce_scatter | solution.py:69
  1633.7 78.7 %copy-start.10 = (bf16[1024,224]{0,1:T(8,128)(2,1)S(1)}, bf16[1024,224]{0,1:T(8,128)(2,1)}, u32[]{:S(2)}) copy-start(bf16[1024,224]{0,1:T(8,128)(2,1)} %param.19) | copy-start | bytes 1376260
  1633.7 122.4 %all-gather.37.cloned.1.call-start = ((), (), s32[]{:S(2)}) async-start(), calls=%async_computation.44 | async-start | bytes 2293760 | tf_op jit(solution)/shard_map/all_gather | solution.py:42
  1714.7 85.6 %reduce-scatter.37.cloned.1.call-start = ((), (), s32[]{:S(2)}) async-start(), calls=%async_computation.45 | async-start | bytes 4587520 | tf_op jit(solution)/shard_map/reduce_scatter | solution.py:55
  1802.3 17.6 all-to-all-start.4
  1806.9 61.6 %all-gather.39.cloned.1.call-start = ((), (), s32[]{:S(2)}) async-start(), calls=%async_computation.46 | async-start | bytes 2949120 | tf_op jit(solution)/shard_map/all_gather | solution.py:46
  1846.1 94.1 %all-gather.31.cloned.1.call-start = ((), (), s32[]{:S(2)}) async-start(), calls=%async_computation.38 | async-start | bytes 13107200 | tf_op jit(solution)/shard_map/all_gather | solution.py:46
  1846.9 164.8 %reduce-scatter.39.cloned.1.call-start = ((), (), s32[]{:S(2)}) async-start(), calls=%async_computation.47 | async-start | bytes 4587520 | tf_op jit(solution)/shard_map/reduce_scatter | solution.py:69
  1873.1 209.6 %reduce-scatter.31.cloned.1.call-start = ((), (), s32[]{:S(2)}) async-start(), calls=%async_computation.39 | async-start | bytes 4587520 | tf_op jit(solution)/shard_map/reduce_scatter | solution.py:69
  1949.3 62.4 %copy-start.56 = (f32[1024]{0:T(1024)S(1)}, f32[1024]{0:T(1024)}, u32[]{:S(2)}) copy-start(f32[1024]{0:T(1024)} %copy-done.55) | copy-start | bytes 12292
  1949.3 62.4 %copy-start.76 = (f32[1,224]{1,0:T(1,128)S(1)}, f32[1,224]{1,0:T(1,128)}, u32[]{:S(2)}) copy-start(f32[1,224]{1,0:T(1,128)} %copy-done.75) | copy-start | bytes 2692
  1949.3 70.0 %copy-start.72 = (f32[1024]{0:T(1024)S(1)}, f32[1024]{0:T(1024)}, u32[]{:S(2)}) copy-start(f32[1024]{0:T(1024)} %copy-done.71) | copy-start | bytes 12292
  1949.3 133.4 %copy-start.50 = (f32[1024]{0:T(1024)S(1)}, f32[1024]{0:T(1024)}, u32[]{:S(2)}) copy-start(f32[1024]{0:T(1024)} %copy-done.49) | copy-start | bytes 12292
  1949.3 133.4 %copy-start.66 = (f32[1024]{0:T(1024)S(1)}, f32[1024]{0:T(1024)}, u32[]{:S(2)}) copy-start(f32[1024]{0:T(1024)} %copy-done.65) | copy-start | bytes 12292
  1949.3 133.4 %copy-start.74 = (f32[1,224]{1,0:T(1,128)S(1)}, f32[1,224]{1,0:T(1,128)}, u32[]{:S(2)}) copy-start(f32[1,224]{1,0:T(1,128)} %copy-done.73) | copy-start | bytes 2692
  1949.4 178.5 %all-gather.41.cloned.1.call-start = ((), (), s32[]{:S(2)}) async-start(), calls=%async_computation.48 | async-start | bytes 2293760 | tf_op jit(solution)/shard_map/all_gather | solution.py:42
  2086.1 202.8 %reduce-scatter.41.cloned.1.call-start = ((), (), s32[]{:S(2)}) async-start(), calls=%async_computation.49 | async-start | bytes 26214400 | tf_op jit(solution)/shard_map/reduce_scatter | solution.py:55
  2139.5 286.2 %all-gather.43.cloned.1.call-start = ((), (), s32[]{:S(2)}) async-start(), calls=%async_computation.50 | async-start | bytes 24903680 | tf_op jit(solution)/shard_map/all_gather | solution.py:46
  2299.7 126.0 %copy-start.9 = (bf16[224,2432]{1,0:T(8,128)(2,1)S(1)}, bf16[224,2432]{1,0:T(8,128)(2,1)}, u32[]{:S(2)}) copy-start(bf16[224,2432]{1,0:T(8,128)(2,1)} %copy-done.8) | copy-start | bytes 3268612
  2299.7 207.0 %reduce-scatter.43.cloned.1.call-start = ((), (), s32[]{:S(2)}) async-start(), calls=%async_computation.51 | async-start | bytes 4587520 | tf_op jit(solution)/shard_map/reduce_scatter | solution.py:69
  2438.0 68.7 %copy-start.54 = (f32[1024]{0:T(1024)S(1)}, f32[1024]{0:T(1024)}, u32[]{:S(2)}) copy-start(f32[1024]{0:T(1024)} %copy-done.53) | copy-start | bytes 12292
  2438.0 68.7 %copy-start.78 = (f32[1,224]{1,0:T(1,128)S(1)}, f32[1,224]{1,0:T(1,128)}, u32[]{:S(2)}) copy-start(f32[1,224]{1,0:T(1,128)} %copy-done.77) | copy-start | bytes 2692
  2438.0 76.3 %copy-start.70 = (f32[1024]{0:T(1024)S(1)}, f32[1024]{0:T(1024)}, u32[]{:S(2)}) copy-start(f32[1024]{0:T(1024)} %copy-done.69) | copy-start | bytes 12292
  2438.0 76.3 %copy-start.11 = (f32[1024,224]{0,1:T(8,128)S(1)}, f32[1024,224]{0,1:T(8,128)}, u32[]{:S(2)}) copy-start(f32[1024,224]{0,1:T(8,128)} %get-tuple-element.130) | copy-start | bytes 2752516
  2438.0 120.3 %copy-start.24 = (bf16[2,224,224]{2,1,0:T(8,128)(2,1)S(1)}, bf16[2,224,224]{2,1,0:T(8,128)(2,1)}, u32[]{:S(2)}) copy-start(bf16[2,224,224]{2,1,0:T(8,128)(2,1)} %param.15) | copy-start | bytes 602116
  2438.0 120.3 %all-gather.45.cloned.1.call-start = ((), (), s32[]{:S(2)}) async-start(), calls=%async_computation.52 | async-start | bytes 2293760 | tf_op jit(solution)/shard_map/all_gather | solution.py:42
  2516.8 85.5 %reduce-scatter.45.cloned.1.call-start = ((), (), s32[]{:S(2)}) async-start(), calls=%async_computation.53 | async-start | bytes 4587520 | tf_op jit(solution)/shard_map/reduce_scatter | solution.py:55
  2604.4 17.5 all-to-all-start.6
  2629.0 21.0 all-to-all-start.7
  2632.5 48.3 %all-gather.47.cloned.1.call-start = ((), (), s32[]{:S(2)}) async-start(), calls=%async_computation.54 | async-start | bytes 2949120 | tf_op jit(solution)/shard_map/all_gather | solution.py:46
  2651.0 137.6 %all-reduce.4.cloned.1.call-start = ((), (), s32[]{:S(2)}) async-start(), calls=%async_computation.56 | async-start | bytes 7929856 | tf_op jit(solution)/shard_map/psum | solution.py:90
  2684.6 174.7 %reduce-scatter.47.cloned.1.call-start = ((), (), s32[]{:S(2)}) async-start(), calls=%async_computation.55 | async-start | bytes 4587520 | tf_op jit(solution)/shard_map/reduce_scatter | solution.py:69
  2794.0 65.3 %copy-start.6 = (bf16[1024,224]{0,1:T(8,128)(2,1)S(1)}, bf16[1024,224]{0,1:T(8,128)(2,1)}, u32[]{:S(2)}) copy-start(bf16[1024,224]{0,1:T(8,128)(2,1)} %param.10) | copy-start | bytes 1376260
  2794.0 65.3 %copy-start.52 = (f32[1024]{0:T(1024)S(1)}, f32[1024]{0:T(1024)}, u32[]{:S(2)}) copy-start(f32[1024]{0:T(1024)} %copy-done.51) | copy-start | bytes 12292
  2794.0 65.3 %copy-start.81 = (f32[1,224]{1,0:T(1,128)S(1)}, f32[1,224]{1,0:T(1,128)}, u32[]{:S(2)}) copy-start(f32[1,224]{1,0:T(1,128)} %copy-done.80) | copy-start | bytes 2692
  2794.1 72.9 %copy-start.68 = (f32[1024]{0:T(1024)S(1)}, f32[1024]{0:T(1024)}, u32[]{:S(2)}) copy-start(f32[1024]{0:T(1024)} %copy-done.67) | copy-start | bytes 12292
  2794.1 72.9 %copy-start.83 = (f32[224]{0:T(256)S(1)}, f32[224]{0:T(256)}, u32[]{:S(2)}) copy-start(f32[224]{0:T(256)} %get-tuple-element.101) | copy-start | bytes 2692
  2794.1 94.5 %copy-start.12 = (f32[1024,224]{0,1:T(8,128)S(1)}, f32[1024,224]{0,1:T(8,128)}, u32[]{:S(2)}) copy-start(f32[1024,224]{0,1:T(8,128)} %get-tuple-element.128) | copy-start | bytes 2752516
  (58 other events, 622.9 us)
Sparse Core Ops, SparseCore 0:
  19.6 41.6 all-gather.16
  66.0 46.5 reduce-scatter.16
  154.8 19.2 all-gather.18
  178.3 68.5 reduce-scatter.18
  255.4 41.3 all-gather.20
  314.2 268.9 reduce-scatter.20
  589.5 70.1 all-gather.22
  668.8 68.5 reduce-scatter.22
  746.0 41.3 all-gather.24
  792.0 46.5 reduce-scatter.24
  879.0 19.2 all-gather.26
  902.4 68.5 reduce-scatter.26
  972.6 41.5 all-gather.32
  1016.2 40.1 all-gather.28
  1058.8 149.3 reduce-scatter.32
  1210.7 270.1 reduce-scatter.28
  1493.1 125.7 all-gather.34
  1633.9 68.5 reduce-scatter.34
  1714.8 41.3 all-gather.36
  1760.3 39.8 reduce-scatter.36
  1846.2 22.1 all-gather.38
  1870.0 70.1 all-gather.30
  1943.1 68.5 reduce-scatter.38
  2013.8 68.8 reduce-scatter.30
  2086.3 41.5 all-gather.40
  2139.6 149.3 reduce-scatter.40
  2299.9 125.7 all-gather.42
  2438.1 68.5 reduce-scatter.42
  2516.9 41.3 all-gather.44
  2562.4 39.8 reduce-scatter.44
  2651.1 24.4 all-gather.46
  2684.7 103.7 all-reduce.3
  2790.7 68.5 reduce-scatter.46
where the time goes:
time: 2910 us; the launch traced here: 2900 us
  waiting for transfers between devices  2400 us (82%)
  matrix products  204 us (7%)
  blocking collectives  147 us (5%)
  other arithmetic  90.5 us (3%)
    reduce_scatter x8, waiting for transfers between devices, reduce_cols(): lax.psum_scatter(block_term(jnp.int32(0), lax.axis_size('col') * share_ro...  987 us
    reduce_scatter x8, waiting for transfers between devices, reduce_rows(): lax.psum_scatter(block_term(jnp.int32(0), lax.axis_size('row') * share_ro...  530 us
    all_gather x8, waiting for transfers between devices, gather_cols(): return lax.all_gather(values, 'col', axis=0, tiled=True)  449 us
    all_gather x8, waiting for transfers between devices, gather_rows(): return lax.all_gather(values, 'row', axis=0, tiled=True)  306 us
    psum x1, waiting for transfers between devices, sum_weights(): lax.psum(as_sent(grad_terms), 'dp')  90.3 us
    dot_general x8, matrix products, multiply(): return jnp.dot(left_rows, right_matrix, preferred_element_type=jnp.float32)  79.7 us
    dot_general x8, matrix products, multiply(): lax.dot_general(left_rows, right_matrix, (((1,), (1,)), ((), ())), prefer...  67.9 us
  transfers between devices with their start and end apart: 37, of which 35 were waited for; matrix products, arithmetic and copies ran while one was open for 5% of the time, Pallas kernels for 0%

commit v1 on v0

v1 whole, which is shorter than its diff:
```python
import math

import jax
import jax.numpy as jnp
from jax import lax
from jax.sharding import PartitionSpec as P

D = 896
HEADS = 14
KV = 2
HEAD = 64
LAYERS = 2
GROUP = HEADS // KV

norm_eps = 1e-06
rope_base = 1000000.0
GRID = ("row", "col")
EVERY = ("dp", "row", "col")


def dot(spec, left, right):
    return jnp.einsum(spec, left, right, preferred_element_type=jnp.float32)


def gather_grid(shard):
    rows = lax.axis_size("row")
    whole = lax.all_gather(shard, GRID, axis=0, tiled=True)
    return whole.reshape(rows, -1, shard.shape[1])


def scatter_grid(blocks):
    flat = blocks.reshape(-1, blocks.shape[-1])
    part = lax.psum_scatter(flat, GRID, scatter_dimension=0, tiled=True)
    return lax.psum(part, "dp")


def per_row(matrix):
    rows = lax.axis_size("row")
    return jnp.broadcast_to(matrix[None], (rows,) + matrix.shape)


def norm_forward(stream, gain):
    inverse = lax.rsqrt(jnp.mean(stream * stream, axis=1, keepdims=True) + norm_eps)
    return ((stream * inverse * gain).astype(jnp.bfloat16), inverse)


def norm_backward(stream, inverse, gain, grad_normed):
    gain_part = jnp.sum(grad_normed * (stream * inverse), axis=0)
    weighted = grad_normed * gain
    inner = jnp.mean(weighted * stream, axis=1, keepdims=True)
    return (weighted * inverse - stream * (inverse * inverse * inverse * inner), gain_part)


def rope_tables(seg_vec):
    index_all = jnp.arange(seg_vec.shape[0], dtype=jnp.int32)
    starts = jnp.concatenate([jnp.ones((1,), jnp.bool_), seg_vec[1:] != seg_vec[:-1]])
    first_idx = lax.cummax(jnp.where(starts, index_all, 0), axis=0)
    positions = (index_all - first_idx).astype(jnp.float32)
    half_dim = HEAD // 2
    freqs = rope_base ** (-(jnp.arange(half_dim, dtype=jnp.float32) * 2.0 / HEAD))
    angles = positions[:, None] * freqs[None, :]
    return (jnp.cos(angles)[:, None, :], jnp.sin(angles)[:, None, :])


def rotate(values, cosine, sine_vals):
    half_dim = values.shape[-1] // 2
    first_half = values[..., :half_dim]
    second_half = values[..., half_dim:]
    return jnp.concatenate(
        [
            first_half * cosine - second_half * sine_vals,
            second_half * cosine + first_half * sine_vals,
        ],
        axis=-1,
    )


def split_heads(qkv, cosine, sine_vals):
    length = qkv.shape[0]
    turned = HEADS + KV
    heads = qkv.reshape(length, turned + KV, HEAD)
    rotated = rotate(heads[:, :turned].astype(jnp.float32), cosine, sine_vals).astype(jnp.bfloat16)
    rotated = jnp.transpose(rotated, (1, 0, 2))
    queries = rotated[:HEADS].reshape(KV, GROUP * length, HEAD)
    return (queries, rotated[HEADS:], jnp.transpose(heads[:, turned:], (1, 0, 2)))


def masked_scores(queries, keys, allowed):
    length = keys.shape[1]
    scores = dot("kqd,ksd->kqs", queries, keys) * (1.0 / math.sqrt(HEAD))
    scores = scores.reshape(KV, GROUP, length, length)
    return jnp.where(allowed[None, None], scores, -1e30)


def attend_forward(heads, allowed):
    queries, keys, values = heads
    length = keys.shape[1]
    scores = masked_scores(queries, keys, allowed)
    row_max = jnp.max(scores, axis=-1, keepdims=True)
    exp_scores = jnp.exp(scores - row_max)
    exp_total = jnp.sum(exp_scores, axis=-1, keepdims=True)
    probs = (exp_scores / exp_total).astype(jnp.bfloat16)
    output = dot("kqs,ksd->kqd", probs.reshape(KV, -1, length), values).astype(jnp.bfloat16)
    output = jnp.transpose(output.reshape(HEADS, length, HEAD), (1, 0, 2))
    return (output.reshape(length, D), row_max + jnp.log(exp_total))


def attend_backward(heads, allowed, log_norm, grad_attn, cosine, sine_vals):
    queries, keys, values = heads
    length = keys.shape[1]
    scale = 1.0 / math.sqrt(HEAD)
    grads = jnp.transpose(grad_attn.reshape(length, HEADS, HEAD), (1, 0, 2))
    grads = grads.reshape(KV, GROUP * length, HEAD)
    probs = jnp.exp(masked_scores(queries, keys, allowed) - log_norm)
    grad_probs = dot("kqd,ksd->kqs", grads, values).reshape(probs.shape)
    inner = jnp.sum(probs * grad_probs, axis=-1, keepdims=True)
    grad_scores = (probs * (grad_probs - inner)).astype(jnp.bfloat16)
    grad_scores = grad_scores.reshape(KV, GROUP * length, length)
    probs = probs.astype(jnp.bfloat16).reshape(KV, GROUP * length, length)
    grad_values = dot("kqs,kqd->ksd", probs, grads)
    grad_keys = dot("kqs,kqd->ksd", grad_scores, queries) * scale
    grad_queries = dot("kqs,ksd->kqd", grad_scores, keys) * scale
    turned = jnp.concatenate([grad_queries.reshape(HEADS, length, HEAD), grad_keys], axis=0)
    turned = rotate(jnp.transpose(turned, (1, 0, 2)), cosine, -sine_vals)
    joined = jnp.concatenate([turned, jnp.transpose(grad_values, (1, 0, 2))], axis=1)
    return joined.reshape(length, -1).astype(jnp.bfloat16)


def silu_product(gate_part, up_part):
    return jax.nn.silu(gate_part) * up_part


def on_device(
    hidden,
    segments,
    attn_gain,
    qkv_weight,
    qkv_bias,
    out_weight,
    mlp_gain,
    gate_up_weight,
    down_weight,
    cotangent,
):
    rows, cols = lax.axis_size("row"), lax.axis_size("col")
    width_dev = qkv_weight.shape[1]
    qkv_dev = qkv_weight.shape[2]
    out_dev = out_weight.shape[1]
    ff_dev = down_weight.shape[1]
    weights = []
    for n in range(LAYERS):
        attn_shard = jnp.concatenate([qkv_weight[n], out_weight[n].T], axis=1)
        weights.append(
            (
                gather_grid(attn_shard),
                gather_grid(gate_up_weight[n].reshape(width_dev, 2 * ff_dev)),
                gather_grid(down_weight[n].T),
            )
        )
    gains = lax.all_gather(jnp.concatenate([attn_gain, mlp_gain]), "col", axis=1, tiled=True)
    gains = gains.astype(jnp.float32)
    biases = lax.all_gather(qkv_bias, "row", axis=1, tiled=True).astype(jnp.float32)
    route = []
    for target in range(rows * cols):
        route.append(((target % rows) * cols + target // rows, target))
    seg_vec = lax.ppermute(segments.reshape(-1), GRID, route)
    both = lax.all_to_all(
        jnp.stack([hidden, cotangent]), "col", split_axis=1, concat_axis=2, tiled=True
    )
    length = both.shape[1]
    cosine, sine_vals = rope_tables(seg_vec)
    index_all = jnp.arange(length, dtype=jnp.int32)
    allowed = (seg_vec[:, None] == seg_vec[None, :]) & (index_all[:, None] >= index_all[None, :])
    stream = both[0].astype(jnp.float32)
    saved = []
    for n in range(LAYERS):
        w_attn, w_gu, w_down = weights[n]
        w_qkv = jnp.transpose(w_attn[:, :, :qkv_dev], (1, 0, 2)).reshape(D, -1)
        w_out = jnp.transpose(w_attn[:, :, qkv_dev:], (1, 0, 2)).reshape(D, -1)
        normed_a, inverse_a = norm_forward(stream, gains[n])
        qkv = (dot("td,df->tf", normed_a, w_qkv) + biases[n]).astype(jnp.bfloat16)
        heads = split_heads(qkv, cosine, sine_vals)
        attended, log_norm = attend_forward(heads, allowed)
        stream_mid = stream + dot("th,dh->td", attended, w_out)
        normed_m, inverse_m = norm_forward(stream_mid, gains[LAYERS + n])
        gate_up = dot("rtd,rdf->rtf", per_row(normed_m), w_gu)
        act = silu_product(gate_up[..., :ff_dev], gate_up[..., ff_dev:]).astype(jnp.bfloat16)
        stream_next = stream_mid + jnp.sum(dot("rtf,rdf->rtd", act, w_down), axis=0)
        saved.append(
            (stream, inverse_a, normed_a, heads, log_norm, attended)
            + (stream_mid, inverse_m, normed_m, gate_up, act, w_qkv, w_out)
        )
        stream = stream_next
    result = stream.astype(jnp.bfloat16)
    grad_stream = both[1].astype(jnp.float32)
    weight_grads = [None] * LAYERS
    small = [None] * (3 * LAYERS)
    for n in reversed(range(LAYERS)):
        _, w_gu, w_down = weights[n]
        stream_in, inverse_a, normed_a, heads, log_norm, attended = saved[n][:6]
        stream_mid, inverse_m, normed_m, gate_up, act, w_qkv, w_out = saved[n][6:]
        grad_down = per_row(grad_stream.astype(jnp.bfloat16))
        grad_act = dot("rtd,rdf->rtf", grad_down, w_down)
        down_term = dot("rtd,rtf->rdf", grad_down, act).astype(jnp.bfloat16)
        down_part = scatter_grid(down_term)
        _, silu_back = jax.vjp(silu_product, gate_up[..., :ff_dev], gate_up[..., ff_dev:])
        grad_gu = jnp.concatenate(silu_back(grad_act), axis=2).astype(jnp.bfloat16)
        gu_term = dot("rtd,rtf->rdf", per_row(normed_m), grad_gu).astype(jnp.bfloat16)
        gu_part = scatter_grid(gu_term)
        grad_normed_m = jnp.sum(dot("rtf,rdf->rtd", grad_gu, w_gu), axis=0)
        grad_norm_m, gain_m = norm_backward(
            stream_mid, inverse_m, gains[LAYERS + n], grad_normed_m
        )
        grad_mid = grad_stream + grad_norm_m
        grad_out = grad_mid.astype(jnp.bfloat16)
        grad_attn = dot("td,dh->th", grad_out, w_out).astype(jnp.bfloat16)
        out_term = dot("td,th->dh", grad_out, attended).astype(jnp.bfloat16)
        grad_qkv = attend_backward(heads, allowed, log_norm, grad_attn, cosine, sine_vals)
        qkv_term = dot("td,tf->df", normed_a, grad_qkv).astype(jnp.bfloat16)
        attn_term = jnp.concatenate(
            [
                jnp.transpose(qkv_term.reshape(D, rows, qkv_dev), (1, 0, 2)),
                jnp.transpose(out_term.reshape(D, rows, out_dev), (1, 0, 2)),
            ],
            axis=2,
        )
        attn_part = scatter_grid(attn_term)
        grad_normed_a = dot("tf,df->td", grad_qkv, w_qkv)
        grad_norm_a, gain_a = norm_backward(stream_in, inverse_a, gains[n], grad_normed_a)
        grad_stream = grad_mid + grad_norm_a
        weight_grads[n] = (attn_part, gu_part, down_part)
        small[n] = gain_a
        small[LAYERS + n] = gain_m
        small[2 * LAYERS + n] = jnp.sum(grad_qkv, axis=0, dtype=jnp.float32)
    outcome = lax.all_to_all(result, "col", split_axis=1, concat_axis=0, tiled=True)
    grad_hidden = lax.all_to_all(grad_stream, "col", split_axis=1, concat_axis=0, tiled=True)
    total = lax.psum(jnp.concatenate(small), EVERY)
    gain_all = total[: 2 * LAYERS * D].reshape(2 * LAYERS, D)
    bias_all = total[2 * LAYERS * D :].reshape(LAYERS, -1)
    gain_dev = lax.dynamic_slice_in_dim(
        gain_all, lax.axis_index("col") * width_dev, width_dev, axis=1
    )
    bias_dev = lax.dynamic_slice_in_dim(bias_all, lax.axis_index("row") * qkv_dev, qkv_dev, axis=1)
    wide = [tuple(part.astype(jnp.float32) for part in parts) for parts in weight_grads]
    return (
        outcome,
        grad_hidden,
        gain_dev[:LAYERS],
        jnp.stack([parts[0][:, :qkv_dev] for parts in wide]),
        bias_dev,
        jnp.stack([parts[0][:, qkv_dev:].T for parts in wide]),
        gain_dev[LAYERS:],
        jnp.stack([parts[1].reshape(width_dev, 2, ff_dev) for parts in wide]),
        jnp.stack([parts[2].T for parts in wide]),
    )


def solution(mesh):
    in_specs = (
        P(("dp", "row"), "col"),
        P("dp", "col", "row", None),
        P(None, "col"),
        P(None, "col", "row"),
        P(None, "row"),
        P(None, "row", "col"),
        P(None, "col"),
        P(None, "col", None, "row"),
        P(None, "row", "col"),
        P(("dp", "row"), "col"),
    )
    out_specs = (
        P(("dp", "row"), "col"),
        P(("dp", "row"), "col"),
        P(None, "col"),
        P(None, "col", "row"),
        P(None, "row"),
        P(None, "row", "col"),
        P(None, "col"),
        P(None, "col", None, "row"),
        P(None, "row", "col"),
    )
    return jax.shard_map(
        on_device, mesh=mesh, in_specs=in_specs, out_specs=out_specs, check_vma=False
    )
```

time: 2910 us -> 1410 us (0.48)
  waiting for transfers between devices: 2400 us -> 949 us
  local copies, waits for them, and re-layouts: 24 us -> 147 us
  blocking collectives: 147 us -> 66.3 us
  other arithmetic: 90.5 us -> 32.7 us
  matrix products: 204 us -> 174 us
    reduce_scatter x16 -> x6, waiting for transfers between devices: 1520 us -> 610 us  [scatter_grid(): part = lax.psum_scatter(flat, GRID, scatter_dimension=0, tiled=True)]
    all_gather x16 -> x6, waiting for transfers between devices: 755 us -> 306 us  [gather_grid(): whole = lax.all_gather(shard, GRID, axis=0, tiled=True)]
    all_to_all x4 -> x0, blocking collectives: 67.9 us -> none  [the longest x3 47.7 us: col_layout(): lax.all_to_all(values, 'row', split_axis=1, concat_axis=0, tiled=True)]
    psum x1, waiting for transfers between devices: 90.3 us -> 29.4 us  [scatter_grid(): return lax.psum(part, 'dp')]
    convert_element_type x0 -> x17, local copies, waits for them, and re-layouts: none -> 39.7 us  [the longest x2 25.5 us: on_device(): down_term = dot('rtd,rtf->rdf', grad_down, act).astype(jnp.bfloat16)]
    transpose x0 -> x13, local copies, waits for them, and re-layouts: none -> 33.2 us  [the longest x4 15.8 us: on_device(): w_qkv = jnp.transpose(w_attn[:, :, :qkv_dev], (1, 0, 2)).reshape(D, -1)]
    psum x10 -> x1, blocking collectives: 79.1 us -> 46.4 us  [on_device(): total = lax.psum(jnp.concatenate(small), EVERY)]
    dot_general x36, matrix products: 204 us -> 174 us  [dot(): return jnp.einsum(spec, left, right, preferred_element_type=jnp.float32)]
  transfers between devices with their start and end apart: 37 -> 17, of which waited for: 35 -> 14; matrix products, arithmetic and copies ran while one was open for 5% -> 18% of each run, Pallas kernels for 0% -> 0%
where the time goes in v1:
time: 1410 us; the launch traced here: 1400 us
  waiting for transfers between devices  949 us (67%)
  matrix products  174 us (12%)
  local copies, waits for them, and re-layouts  147 us (10%)
  blocking collectives  66.3 us (5%)
  other arithmetic  32.7 us (2%)
  starting transfers between devices  17.8 us (1%)
  between operations  15.6 us (1%)
    reduce_scatter x6, waiting for transfers between devices, scatter_grid(): part = lax.psum_scatter(flat, GRID, scatter_dimension=0, tiled=True)  610 us
    all_gather x6, waiting for transfers between devices, gather_grid(): whole = lax.all_gather(shard, GRID, axis=0, tiled=True)  306 us
    dot_general x36, matrix products, dot(): return jnp.einsum(spec, left, right, preferred_element_type=jnp.float32)  174 us
    psum x1, blocking collectives, on_device(): total = lax.psum(jnp.concatenate(small), EVERY)  46.4 us
    psum x1, waiting for transfers between devices, scatter_grid(): return lax.psum(part, 'dp')  29.4 us
  transfers between devices with their start and end apart: 17, of which 14 were waited for; matrix products, arithmetic and copies ran while one was open for 18% of the time, Pallas kernels for 0%

profile of v1, /device:TPU:0, one launch (start us, length us, event | category | flops | bytes accessed | tf_op | source)
XLA Modules:
  0.0 1402.4 jit_solution(16745656117175734269)
XLA Ops:
  11.5 2.9 fusion.79
  22.4 8.8 all-to-all-start
  31.2 12.0 all-gather.1
  43.3 7.9 all-gather
  58.7 5.7 all-gather.9.cloned.1.call-done
  64.4 3.6 slice_bitcast_fusion.1
  67.9 4.3 copy.367
  72.3 3.6 slice_bitcast_fusion.3
  75.9 2.8 copy.375
  78.8 3.9 fusion.14
  88.2 25.5 %all-gather.15.cloned.1.call-done = bf16[3584,512]{1,0:T(8,128)(2,1)} async-done(((bf16[224,512]{1,0:T(8,128)(2,1)}), bf16[3584,512]{1,0:T(8,128)(2,1)}) %all-gather.15.cloned.1.call-update) | async-done | bytes 3670032 | tf_op jit(solution)/shard_map/all_gather | solution.py:27
  113.7 3.6 slice_bitcast_fusion
  117.2 4.3 copy.384
  121.6 3.6 slice_bitcast_fusion.2
  125.2 3.6 copy.391
  136.3 69.8 %all-gather.11.cloned.1.call-done = bf16[3584,2432]{1,0:T(8,128)(2,1)} async-done(((bf16[224,2432]{1,0:T(8,128)(2,1)}), bf16[3584,2432]{1,0:T(8,128)(2,1)}) %all-gather.11.cloned.1.call-update) | async-done | bytes 17432592 | tf_op jit(solution)/shard_map/all_gather | solution.py:27
  206.1 13.2 fusion.46
  219.3 4.7 multiply_convert_fusion.3
  224.0 63.5 %all-gather.13.cloned.1.call-done = bf16[3584,1216]{1,0:T(8,128)(2,1)} async-done(((bf16[224,1216]{1,0:T(8,128)(2,1)}), bf16[3584,1216]{1,0:T(8,128)(2,1)}) %all-gather.13.cloned.1.call-update) | async-done | bytes 8716304 | tf_op jit(solution)/shard_map/all_gather | solution.py:27
  287.5 7.0 multiply_reduce_fusion.11
  305.6 73.9 %all-gather.17.cloned.1.call-done = bf16[3584,2432]{1,0:T(8,128)(2,1)} async-done(((bf16[224,2432]{1,0:T(8,128)(2,1)}), bf16[3584,2432]{1,0:T(8,128)(2,1)}) %all-gather.17.cloned.1.call-update) | async-done | bytes 17432592 | tf_op jit(solution)/shard_map/all_gather | solution.py:27
  379.5 13.3 fusion.43
  392.9 68.1 %all-gather.19.cloned.1.call-done = bf16[3584,1216]{1,0:T(8,128)(2,1)} async-done(((bf16[224,1216]{1,0:T(8,128)(2,1)}), bf16[3584,1216]{1,0:T(8,128)(2,1)}) %all-gather.19.cloned.1.call-update) | async-done | bytes 8716304 | tf_op jit(solution)/shard_map/all_gather | solution.py:27
  460.9 14.8 %fusion.2 = (bf16[4,256,1216]{1,2,0:T(8,128)(2,1)}, bf16[4,256,1216]{1,2,0:T(8,128)(2,1)}, bf16[4,256,1216]{1,2,0:T(8,128)(2,1)}) fusion(f32[4,256,2432]{1,2,0:T(8,128)} %fusion.43, bf16[4,896,1216]{2,1,0:T(8,128)(2,1)} %bitcast.277, bf16[256,896]{1,0:T(8,128)(2,1)S(1)} %copy-done.22), kind=kOutput, calls=%fused_computation.8 | convolution fusion | flops 2251292672 | bytes 26607616 | tf_op jit(solution)/shard_map/rtd,rdf->rtf/dot_general | solution.py:22
  475.7 12.9 multiply_reduce_fusion.2
  490.3 2.9 convolution_convert_fusion.11
  496.8 2.8 fusion.27
  506.3 2.9 reshape.539
  513.9 14.2 %fusion.5 = (bf16[4,256,1216]{1,2,0:T(8,128)(2,1)}, bf16[4,256,1216]{1,2,0:T(8,128)(2,1)}) fusion(f32[4,256,2432]{1,2,0:T(8,128)} %fusion.46, bf16[4,896,1216]{2,1,0:T(8,128)(2,1)} %bitcast.280, bf16[256,896]{1,0:T(8,128)(2,1)S(1)} %get-tuple-element.69), kind=kOutput, calls=%fused_computation.11 | convolution fusion | flops 2248802304 | bytes 24117248 | tf_op jit(solution)/shard_map/rtd,rdf->rtf/dot_general | solution.py:22
  528.1 11.3 convolution_convert_fusion.1
  539.4 14.0 convolution_convert_fusion
  553.5 2.2 convolution_convert_fusion.4
  555.7 4.3 copy.432
  561.9 2.3 pad_maximum_fusion.3
  564.3 6.1 copy.433
  571.5 12.9 multiply_reduce_fusion.3
  587.6 3.1 multiply_reduce_fusion
  594.4 2.9 reshape.542
  602.9 2.1 convolution_convert_fusion.5
  605.1 2.9 copy.430
  609.7 2.1 pad_maximum_fusion.2
  611.8 6.1 copy.431
  618.9 7.9 convolution_convert_fusion.2
  626.8 12.7 copy.437
  641.2 6.1 convolution_convert_fusion.3
  647.3 12.8 copy.436
  660.1 61.3 %reduce-scatter.11.cloned.1.call-done = bf16[224,2432]{1,0:T(8,128)(2,1)} async-done(((bf16[3584,2432]{1,0:T(8,128)(2,1)}), bf16[224,2432]{1,0:T(8,128)(2,1)}) %reduce-scatter.11.cloned.1.call-update) | async-done | bytes 1089552 | tf_op jit(solution)/shard_map/reduce_scatter | solution.py:33
  721.4 3.0 stack_reshape.8
  724.5 183.7 %reduce-scatter.13.cloned.1.call-done = bf16[224,2432]{1,0:T(8,128)(2,1)} async-done(((bf16[3584,2432]{1,0:T(8,128)(2,1)}), bf16[224,2432]{1,0:T(8,128)(2,1)}) %reduce-scatter.13.cloned.1.call-update) | async-done | bytes 1089552 | tf_op jit(solution)/shard_map/reduce_scatter | solution.py:33
  908.2 3.0 stack_reshape.9
  911.2 68.6 %reduce-scatter.9.cloned.1.call-done = bf16[224,512]{1,0:T(8,128)(2,1)} async-done(((bf16[3584,512]{1,0:T(8,128)(2,1)}), bf16[224,512]{1,0:T(8,128)(2,1)}) %reduce-scatter.9.cloned.1.call-update) | async-done | bytes 229392 | tf_op jit(solution)/shard_map/reduce_scatter | solution.py:33
  979.8 71.3 %reduce-scatter.7.cloned.1.call-done = bf16[224,512]{1,0:T(8,128)(2,1)} async-done(((bf16[3584,512]{1,0:T(8,128)(2,1)}), bf16[224,512]{1,0:T(8,128)(2,1)}) %reduce-scatter.7.cloned.1.call-update) | async-done | bytes 229392 | tf_op jit(solution)/shard_map/reduce_scatter | solution.py:33
  1051.0 112.4 %reduce-scatter.17.cloned.1.call-done = bf16[224,1216]{1,0:T(8,128)(2,1)} async-done(((bf16[3584,1216]{1,0:T(8,128)(2,1)}), bf16[224,1216]{1,0:T(8,128)(2,1)}) %reduce-scatter.17.cloned.1.call-update) | async-done | bytes 544784 | tf_op jit(solution)/shard_map/reduce_scatter | solution.py:33
  1163.5 113.1 %reduce-scatter.15.cloned.1.call-done = bf16[224,1216]{1,0:T(8,128)(2,1)} async-done(((bf16[3584,1216]{1,0:T(8,128)(2,1)}), bf16[224,1216]{1,0:T(8,128)(2,1)}) %reduce-scatter.15.cloned.1.call-update) | async-done | bytes 544784 | tf_op jit(solution)/shard_map/reduce_scatter | solution.py:33
  1276.7 8.2 fusion.26
  1284.8 2.2 copy.397
  1287.0 4.1 all-to-all-start.1
  1291.2 2.6 multiply_reduce_fusion.5
  1294.9 2.4 copy.427
  1299.3 3.5 all-to-all-start.2
  1303.0 46.4 %psum.49 = f32[5888]{0:T(1024)S(1)} all-reduce(f32[5888]{0:T(1024)S(1)} %constant_dynamic-update-slice_fusion), channel_id=1, replica_groups=mesh['dp'=2,'row'=4,'col'=4] {'dp','row','col'}, use_global_device_ids=true, to_apply=%region_22.23 | all-reduce | flops 5888 | bytes 47104 | tf_op jit(solution)/shard_map/psum | solution.py:237
  1353.7 29.4 %all-reduce.3.cloned.1.call-done = (bf16[224,512]{1,0:T(8,128)(2,1)}, bf16[224,512]{1,0:T(8,128)(2,1)}, bf16[1,224,2,1216]{3,2,1,0:T(2,128)(2,1)}, bf16[1,224,2,...) async-done(((bf16[224,512]{1,0:T(8,128)(2,1)}, bf16[224,512]{1,0:T(8,128)(2,1)}, bf16[1,224,2,1216]{3,2,1,0:T(2,128)(2,1)}, ...) | async-done | bytes 3727376 | tf_op jit(solution)/shard_map/psum | solution.py:34
  1387.4 2.8 maximum_convert_fusion.2
  1390.2 5.2 maximum_convert_fusion
  (298 shorter events, 91.8 us)
Async XLA Ops:
  7.2 57.2 %all-gather.9.cloned.1.call-start = ((), (), s32[]{:S(2)}) async-start(), calls=%async_computation.9 | async-start | bytes 3899392 | tf_op jit(solution)/shard_map/all_gather | solution.py:27
  10.3 103.4 %all-gather.15.cloned.1.call-start = ((), (), s32[]{:S(2)}) async-start(), calls=%async_computation.12 | async-start | bytes 3899392 | tf_op jit(solution)/shard_map/all_gather | solution.py:27
  11.4 4.7 copy-start.41
  11.4 194.7 %all-gather.11.cloned.1.call-start = ((), (), s32[]{:S(2)}) async-start(), calls=%async_computation.10 | async-start | bytes 18522112 | tf_op jit(solution)/shard_map/all_gather | solution.py:27
  16.0 3.5 copy-start.63
  16.0 4.2 copy-start.42
  16.0 4.2 copy-start.43
  16.1 271.4 %all-gather.13.cloned.1.call-start = ((), (), s32[]{:S(2)}) async-start(), calls=%async_computation.11 | async-start | bytes 9748480 | tf_op jit(solution)/shard_map/all_gather | solution.py:27
  17.2 362.3 %all-gather.17.cloned.1.call-start = ((), (), s32[]{:S(2)}) async-start(), calls=%async_computation.13 | async-start | bytes 18522112 | tf_op jit(solution)/shard_map/all_gather | solution.py:27
  19.0 12.2 copy-start.60
  19.0 24.3 %copy-start.61 = (bf16[2,224]{1,0:T(2,128)(2,1)S(1)}, bf16[2,224]{1,0:T(2,128)(2,1)}, u32[]{:S(2)}) copy-start(bf16[2,224]{1,0:T(2,128)(2,1)} %param.16) | copy-start | bytes 2692
  19.0 24.3 %copy-start.62 = (bf16[2,224]{1,0:T(2,128)(2,1)S(1)}, bf16[2,224]{1,0:T(2,128)(2,1)}, u32[]{:S(2)}) copy-start(bf16[2,224]{1,0:T(2,128)(2,1)} %param.12) | copy-start | bytes 2692
  19.0 441.9 %all-gather.19.cloned.1.call-start = ((), (), s32[]{:S(2)}) async-start(), calls=%async_computation.14 | async-start | bytes 9748480 | tf_op jit(solution)/shard_map/all_gather | solution.py:27
  19.6 32.5 %collective-permute-start = (s32[256]{0:T(256)S(1)}, s32[256]{0:T(256)S(1)}, u32[]{:S(2)}, u32[]{:S(2)}) collective-permute-start(s32[256]{0:T(256)S(1)} %bitcast.281), channel_id=1, source_target_pairs={{0,0},{4,1},{8,2},{12,3},{1,4},{5,5},{9,6},{13,7},{2,8},{6,9},{10,... | collective-permute-start | bytes 3080 | tf_op jit(solution)/shard_map/ppermute | solution.py:166
  22.4 33.0 %all-to-all-start = ((bf16[2,1024,224]{2,0,1:T(2,128)(2,1)}), bf16[2,1024,224]{2,0,1:T(2,128)(2,1)S(1)}, u32[]{:S(2)}, u32[]{:S(2)}) async-start(bf16[2,1024,224]{2,0,1:T(2,128)(2,1)} %copy.360), calls=%async_computation | async-start | bytes 2097152 | tf_op jit(solution)/shard_map/all_to_all | solution.py:167
  31.2 690.3 %reduce-scatter.11.cloned.1.call-start = ((), (), s32[]{:S(2)}) async-start(), calls=%async_computation.17 | async-start | bytes 18522112 | tf_op jit(solution)/shard_map/reduce_scatter | solution.py:33
  52.0 5.6 copy-start.48
  55.4 28.7 %copy-start.46 = (f32[256,32]{0,1:T(8,128)}, f32[256,32]{0,1:T(8,128)S(1)}, u32[]{:S(2)}) copy-start(f32[256,32]{0,1:T(8,128)S(1)} %get-tuple-element.97) | copy-start | bytes 98308
  57.6 76.6 %copy-start.9 = (f32[256,896]{1,0:T(8,128)}, f32[256,896]{1,0:T(8,128)S(1)}, u32[]{:S(2)}) copy-start(f32[256,896]{1,0:T(8,128)S(1)} %copy.376) | copy-start | bytes 2752516
  58.5 13.8 copy-start.54
  58.7 20.1 %copy-start.35 = (bf16[1,256,4,224]{1,3,2,0:T(8,128)(2,1)}, bf16[1,256,4,224]{1,3,2,0:T(8,128)(2,1)S(1)}, u32[]{:S(2)}) copy-start(bf16[1,256,4,224]{1,3,2,0:T(8,128)(2,1)S(1)} %multiply_convert_fusion.9) | copy-start | bytes 1376260
  78.7 55.4 %copy-start.11 = (bf16[896,4,224]{0,2,1:T(8,128)(2,1)}, bf16[896,4,224]{0,2,1:T(8,128)(2,1)S(1)}, u32[]{:S(2)}) copy-start(bf16[896,4,224]{0,2,1:T(8,128)(2,1)S(1)} %copy.375) | copy-start | bytes 4816900
  84.0 47.4 %copy-start.31 = (bf16[256,1152]{0,1:T(8,128)(2,1)}, bf16[256,1152]{0,1:T(8,128)(2,1)S(1)}, u32[]{:S(2)}) copy-start(bf16[256,1152]{0,1:T(8,128)(2,1)S(1)} %copy.369) | copy-start | bytes 1769476
  130.8 2.4 copy-start
  224.0 70.5 %copy-start.5 = (bf16[4,256,1216]{1,2,0:T(8,128)(2,1)}, bf16[4,256,1216]{1,2,0:T(8,128)(2,1)S(1)}, u32[]{:S(2)}) copy-start(bf16[4,256,1216]{1,2,0:T(8,128)(2,1)S(1)} %multiply_convert_fusion.3) | copy-start | bytes 7471108
  287.5 7.9 copy-start.14
  287.5 7.9 copy-start.58
  294.5 2.2 copy-start.47
  296.6 2.7 copy-start.32
  296.9 1.8 copy-start.34
  298.8 1.8 copy-start.3
  299.3 4.1 copy-start.8
  300.6 2.8 copy-start.13
  379.5 81.4 %copy-start.22 = (bf16[256,896]{1,0:T(8,128)(2,1)S(1)}, bf16[256,896]{1,0:T(8,128)(2,1)}, u32[]{:S(2)}) copy-start(bf16[256,896]{1,0:T(8,128)(2,1)} %copy.399) | copy-start | bytes 1376260
  460.9 14.8 %copy-start.18 = (f32[256,896]{1,0:T(8,128)S(1)}, f32[256,896]{1,0:T(8,128)}, u32[]{:S(2)}) copy-start(f32[256,896]{1,0:T(8,128)} %copy-done.17) | copy-start | bytes 2752516
  496.7 3.1 copy-start.4
  504.6 6.6 copy-start.45
  509.1 2.4 copy-start.15
  513.9 14.2 %copy-start.26 = (bf16[256,896]{1,0:T(8,128)(2,1)}, bf16[256,896]{1,0:T(8,128)(2,1)S(1)}, u32[]{:S(2)}) copy-start(bf16[256,896]{1,0:T(8,128)(2,1)S(1)} %get-tuple-element.69) | copy-start | bytes 1376260
  539.4 368.8 %reduce-scatter.13.cloned.1.call-start = ((), (), s32[]{:S(2)}) async-start(), calls=%async_computation.18 | async-start | bytes 18522112 | tf_op jit(solution)/shard_map/reduce_scatter | solution.py:33
  553.4 6.6 copy-start.29
  553.4 426.4 %reduce-scatter.9.cloned.1.call-start = ((), (), s32[]{:S(2)}) async-start(), calls=%async_computation.16 | async-start | bytes 3899392 | tf_op jit(solution)/shard_map/reduce_scatter | solution.py:33
  560.0 1.9 copy-start.16
  570.4 480.7 %reduce-scatter.7.cloned.1.call-start = ((), (), s32[]{:S(2)}) async-start(), calls=%async_computation.15 | async-start | bytes 3899392 | tf_op jit(solution)/shard_map/reduce_scatter | solution.py:33
  571.5 12.9 copy-start.30
  584.4 1.7 copy-start.12
  587.6 3.2 copy-start.1
  597.3 3.9 copy-start.2
  601.0 1.9 copy-start.36
  617.9 545.6 %reduce-scatter.17.cloned.1.call-start = ((), (), s32[]{:S(2)}) async-start(), calls=%async_computation.20 | async-start | bytes 9748480 | tf_op jit(solution)/shard_map/reduce_scatter | solution.py:33
  639.5 1.7 copy-start.6
  639.5 637.1 %reduce-scatter.15.cloned.1.call-start = ((), (), s32[]{:S(2)}) async-start(), calls=%async_computation.19 | async-start | bytes 9748480 | tf_op jit(solution)/shard_map/reduce_scatter | solution.py:33
  660.1 616.5 %copy-start.19 = (f32[256,896]{1,0:T(8,128)S(1)}, f32[256,896]{1,0:T(8,128)}, u32[]{:S(2)}) copy-start(f32[256,896]{1,0:T(8,128)} %copy-done.17) | copy-start | bytes 2752516
  660.1 723.0 %all-reduce.3.cloned.1.call-start = ((), (), s32[]{:S(2)}) async-start(), calls=%async_computation.21 | async-start | bytes 7798784 | tf_op jit(solution)/shard_map/psum | solution.py:34
  1276.6 14.5 %copy-start.10 = (f32[256,896]{1,0:T(8,128)S(1)}, f32[256,896]{1,0:T(8,128)}, u32[]{:S(2)}) copy-start(f32[256,896]{1,0:T(8,128)} %copy-done.9) | copy-start | bytes 2752516
  1276.6 14.5 %copy-start.25 = (bf16[256,18,64]{0,2,1:T(8,128)(2,1)S(1)}, bf16[256,18,64]{0,2,1:T(8,128)(2,1)}, u32[]{:S(2)}) copy-start(bf16[256,18,64]{0,2,1:T(8,128)(2,1)} %copy-done.24) | copy-start | bytes 1769476
  1276.6 14.5 %copy-start.49 = (f32[896]{0:T(1024)S(1)}, f32[896]{0:T(1024)}, u32[]{:S(2)}) copy-start(f32[896]{0:T(1024)} %copy-done.48) | copy-start | bytes 10756
  1276.6 14.5 %copy-start.55 = (f32[256]{0:T(256)S(1)}, f32[256]{0:T(256)}, u32[]{:S(2)}) copy-start(f32[256]{0:T(256)} %copy-done.54) | copy-start | bytes 3076
  1284.8 8.9 copy-start.57
  1287.0 12.3 all-to-all-start.1
  1293.8 9.2 copy-start.59
  1299.3 53.3 %all-to-all-start.2 = ((f32[256,4,224]{0,2,1:T(8,128)}), f32[256,4,224]{0,2,1:T(8,128)S(1)}, u32[]{:S(2)}, u32[]{:S(2)}) async-start(f32[256,4,224]{0,2,1:T(8,128)} %bitcast.67), calls=%async_computation.2 | async-start | bytes 1835008 | tf_op jit(solution)/shard_map/all_to_all | solution.py:236
  1385.3 4.9 copy-start.39
  1385.3 4.9 copy-start.40
  (17 other events, 15.9 us)
Sparse Core Ops, SparseCore 0:
  10.8 53.4 all-gather.8
  67.2 46.4 all-gather.14
  115.3 90.7 all-gather.10
  208.2 79.2 all-gather.12
  288.9 90.5 all-gather.16
  381.7 79.2 all-gather.18
  539.5 181.8 reduce-scatter.10
  725.6 182.5 reduce-scatter.12
  912.0 67.7 reduce-scatter.8
  983.5 67.5 reduce-scatter.6
  1055.2 108.2 reduce-scatter.16
  1167.5 109.0 reduce-scatter.14
  1279.8 103.2 all-reduce.2
